TPU v7x, 32 devices: a whole 2x2x4 slice. The times are simulated.
32 devices in a mesh: blk: 8 (over z, y), pix: 4 (over x, core).
Axes of the slice: x: 2, y: 2, z: 4, core: 2. Of those that a mesh axis runs over, the one named last changes fastest.
Arguments:
- images: bfloat16 [256, 16384], P('blk', 'pix'), may hold values from -14 to 14
- templates: bfloat16 [2304, 16384], P('blk', 'pix'), may hold values from -4 to 4
- routes: int32 [256, 4], P('blk'), may hold values from 0 to 7, all different within a row; in each aligned block of 32 rows (0 to 31, 32 to 63, ...) at most 24 rows name the same one
- image_weight: float32 [256], P('blk'), may hold values from 0.25 to 4
- template_weight: float32 [2304], P('blk'), may hold values from 0.25 to 4
Outputs:
- template_means: bfloat16 [2304, 16384], P('blk', 'pix')
- image_duals: float32 [256], P('blk')
Inputs may be any that keep to these rules, and one draw needn't show every extreme that they name: `routes`: each image names 4 different template blocks. Among the 32 images of one block, at most 24 name any one template block, and some template block is named by exactly 24 of them. Every template block is named by some image.
All inputs are finite; a program needn't handle non-finite values.
Results may differ from a plain program's by a relative error of at most 0.0046.
Values may be sent and summed in bfloat16 or wider, within the bound.
A program may use at most 64 MiB of HBM per device.

v0:
```python
import jax
import jax.numpy as jnp
from jax import lax
from jax.sharding import PartitionSpec as P

SWEEPS = 2


def on_device(images, templates, routes, image_weight, template_weight):
    blocks = lax.axis_size("blk")
    img_dev = images.shape[0]
    admits = routes.shape[1]
    capacity = max(2, (3 * img_dev * admits + 2 * blocks - 1) // (2 * blocks))
    target = routes.reshape(-1)
    target_hot = (target[:, None] == jnp.arange(blocks, dtype=jnp.int32)[None, :]).astype(jnp.int32)
    before = jnp.cumsum(target_hot, axis=0) - target_hot
    position = jnp.sum(before * target_hot, axis=1)
    slot_of = target * capacity + position
    wanted = jnp.arange(blocks * capacity, dtype=jnp.int32)
    matches = slot_of[None, :] == wanted[:, None]
    filled = jnp.any(matches, axis=1)
    owner_image = jnp.sum(
        jnp.where(matches, jnp.arange(target.shape[0], dtype=jnp.int32)[None, :] // admits, 0),
        axis=1,
    )
    outgoing = jnp.where(filled[:, None], images[owner_image], jnp.zeros((), images.dtype))
    outgoing = outgoing.reshape(blocks, capacity, images.shape[1])
    slot_flags = filled.astype(jnp.bfloat16).reshape(blocks, capacity)
    template_log = jnp.log(template_weight)
    arrived_piece = lax.all_to_all(outgoing, "blk", split_axis=0, concat_axis=0, tiled=True)
    marks_piece = lax.all_to_all(slot_flags, "blk", split_axis=0, concat_axis=0, tiled=True)
    partial_value = jnp.einsum(
        "bmp,tp->bmt", arrived_piece, templates, preferred_element_type=jnp.float32
    )
    summed = lax.psum(partial_value, "pix")
    usable = marks_piece > 0
    image_log = jnp.log(image_weight)
    slot_duals = jnp.zeros((blocks, capacity), jnp.float32)
    image_duals = jnp.zeros((img_dev,), jnp.float32)
    for sweep_index in range(SWEEPS):
        column_terms = jnp.where(usable[:, :, None], summed + slot_duals[:, :, None], -jnp.inf)
        column_peak = jnp.max(column_terms, axis=(0, 1))
        template_duals = (
            template_log
            - column_peak
            - jnp.log(jnp.sum(jnp.exp(column_terms - column_peak), axis=(0, 1)))
        )
        row_terms = summed + template_duals
        row_peak = jnp.max(row_terms, axis=2)
        row_total = jnp.sum(jnp.exp(row_terms - row_peak[:, :, None]), axis=2)
        levels = row_peak + jnp.log(row_total)
        back_levels = lax.all_to_all(levels, "blk", split_axis=0, concat_axis=0, tiled=True)
        level_routes = back_levels.reshape(-1)[slot_of].reshape(img_dev, admits)
        route_peak = jnp.max(level_routes, axis=1)
        image_duals = (
            image_log
            - route_peak
            - jnp.log(jnp.sum(jnp.exp(level_routes - route_peak[:, None]), axis=1))
        )
        duals_send = jnp.where(filled, image_duals[owner_image], 0.0).reshape(blocks, capacity)
        slot_duals = lax.all_to_all(duals_send, "blk", split_axis=0, concat_axis=0, tiled=True)
    column_terms = jnp.where(usable[:, :, None], summed + slot_duals[:, :, None], -jnp.inf)
    column_peak = jnp.max(column_terms, axis=(0, 1))
    column_exp = jnp.exp(column_terms - column_peak)
    plan_weights = (column_exp / jnp.sum(column_exp, axis=(0, 1))).astype(jnp.bfloat16)
    template_means = jnp.einsum(
        "bmt,bmp->tp", plan_weights, arrived_piece, preferred_element_type=jnp.float32
    ).astype(jnp.bfloat16)
    return (template_means, image_duals)


def solution(mesh):
    in_specs = (P("blk", "pix"), P("blk", "pix"), P("blk", None), P("blk"), P("blk"))
    out_specs = (P("blk", "pix"), P("blk"))
    return jax.shard_map(
        on_device, mesh=mesh, in_specs=in_specs, out_specs=out_specs, check_vma=False
    )
```

profile of v0, /device:TPU:0, one launch (start us, length us, event | category | flops | bytes accessed | tf_op | source)
XLA Modules:
  0.0 203.8 jit_solution(13468316568536961378)
XLA Ops:
  7.2 0.9 copy.17
  9.0 2.7 %gather_fusion = bf16[192,4096]{1,0:T(8,128)(2,1)} fusion(bf16[32,4096]{1,0:T(8,128)(2,1)S(1)} %copy-done.1, s32[1024]{0:T(1024)S(1)} %pad_clamp_fusion.1), kind=kCustom, calls=%fused_computation | custom fusion | bytes 3146496 | tf_op jit(solution)/shard_map/gather | solution.py:26
  11.7 2.7 %broadcast_select_fusion = bf16[8,24,4096]{2,1,0:T(8,128)(2,1)} fusion(bf16[8,24,4096]{2,1,0:T(8,128)(2,1)} %bitcast.88, pred[8,24]{1,0:T(8,128)(4,1)S(1)} %broadcast_in_dim.77), kind=kLoop, calls=%fused_computation.7 | loop fusion | flops 786432 | bytes 3145920 | tf_op jit(solution)/shard_map/jit(_where)/select_n | solution.py:26
  14.4 7.4 %all-to-all-start.1 = ((bf16[8,24,4096]{2,1,0:T(8,128)(2,1)}), bf16[8,24,4096]{2,1,0:T(8,128)(2,1)}, u32[]{:S(2)}, u32[]{:S(2)}) async-start(bf16[8,24,4096]{2,1,0:T(8,128)(2,1)} %broadcast_select_fusion), calls=%async_computation.1 | async-start | bytes 3145728 | tf_op jit(solution)/shard_map/all_to_all | solution.py:30
  22.1 0.7 reshape.347
  22.8 36.2 %all-to-all-done.1 = bf16[8,24,4096]{2,1,0:T(8,128)(2,1)} async-done(((bf16[8,24,4096]{2,1,0:T(8,128)(2,1)}), bf16[8,24,4096]{2,1,0:T(8,128)(2,1)}, u32[]{:S(2)}, u32[]{:S(2)}) %all-to-all-start.1) | async-done | bytes 1572896 | tf_op jit(solution)/shard_map/all_to_all | solution.py:30
  59.0 3.6 %all-to-all-start = ((bf16[8,1,24]{2,1,0:T(2,128)(2,1)}), bf16[8,1,24]{2,1,0:T(2,128)(2,1)S(1)}, u32[]{:S(2)}, u32[]{:S(2)}) async-start(bf16[8,1,24]{2,1,0:T(2,128)(2,1)} %reshape.347), calls=%async_computation | async-start | bytes 8192 | tf_op jit(solution)/shard_map/all_to_all | solution.py:31
  62.7 3.3 %fusion.1 = f32[8,24,288]{2,1,0:T(8,128)} fusion(bf16[8,24,4096]{2,1,0:T(8,128)(2,1)} %all-to-all-done.1, bf16[288,4096]{1,0:T(8,128)(2,1)S(1)} %copy-done), kind=kOutput, calls=%fused_computation.5 | convolution fusion | flops 452984832 | bytes 4153344 | tf_op jit(solution)/shard_map/bmp,tp->bmt/dot_general | solution.py:32
  66.0 3.1 %all-to-all-done = bf16[8,1,24]{2,1,0:T(2,128)(2,1)S(1)} async-done(((bf16[8,1,24]{2,1,0:T(2,128)(2,1)}), bf16[8,1,24]{2,1,0:T(2,128)(2,1)S(1)}, u32[]{:S(2)}, u32[]{:S(2)}) %all-to-all-start) | async-done | bytes 416 | tf_op jit(solution)/shard_map/all_to_all | solution.py:31
  69.1 31.1 %all-reduce.2.cloned.1.call-done = f32[8,24,288]{2,1,0:T(8,128)} async-done(((f32[8,24,288]{2,1,0:T(8,128)}), f32[8,24,288]{2,1,0:T(8,128)}) %all-reduce.2.cloned.1.call-update) | async-done | bytes 221200 | tf_op jit(solution)/shard_map/psum | solution.py:35
  100.2 1.1 select_reduce_fusion
  101.3 1.1 exponential_reduce_fusion.3
  102.5 1.1 add_reduce_fusion.1
  103.5 1.2 exponential_reduce_fusion.2
  104.7 0.6 log_add_fusion.1
  105.3 5.5 %all-to-all-start.2 = ((f32[8,1,24]{2,1,0:T(1,128)}), f32[8,1,24]{2,1,0:T(1,128)S(1)}, u32[]{:S(2)}, u32[]{:S(2)}) async-start(f32[8,1,24]{2,1,0:T(1,128)} %bitcast.5), calls=%async_computation.2 | async-start | bytes 8192 | tf_op jit(solution)/shard_map/all_to_all | solution.py:52
  110.8 6.4 %all-to-all-done.2 = f32[8,1,24]{2,1,0:T(1,128)S(1)} async-done(((f32[8,1,24]{2,1,0:T(1,128)}), f32[8,1,24]{2,1,0:T(1,128)S(1)}, u32[]{:S(2)}, u32[]{:S(2)}) %all-to-all-start.2) | async-done | bytes 800 | tf_op jit(solution)/shard_map/all_to_all | solution.py:52
  117.2 0.5 broadcast.505
  117.7 0.7 reduce.6
  118.5 1.3 gather_fusion.1
  120.2 0.7 fusion.18
  120.9 0.7 fusion.17
  121.6 19.9 %select_select_fusion.1 = f32[192]{0:T(256)S(1)} fusion(pred[192]{0:T(512)(128)(4,1)S(1)} %fusion.11, f32[]{:T(128)} %bitcast.8, f32[]{:T(128)} %bitcast.9, f32[]{:T(128)} %bitcast.10, f32[]{:T(128)} %bitcast.11, f32[]{:T(128)} %bitcast.12, f32[]{:T(128)} %bitcast.13, f32[]{:T(128)} %bitcast.14, f32[]{:T(128)} %bitcast.15, f32[]{:T(128)} %bitcast.16, ...), kind=kLoop, calls=%fused_computation.46 | loop fusion | flops 12096 | bytes 1856 | tf_op jit(solution)/shard_map/jit(_where)/select_n | solution.py:60
  141.6 8.8 %all_to_all.35 = f32[8,1,24]{2,1,0:T(1,128)S(1)} all-to-all(f32[8,1,24]{2,1,0:T(1,128)S(1)} %select_n.88), channel_id=1, replica_groups=mesh['blk'=8,'pix'=4] {'blk'}, dimensions={0} | all-to-all | bytes 1536 | tf_op jit(solution)/shard_map/all_to_all | solution.py:61
  151.1 8.9 %all_to_all.36 = f32[8,1,24]{2,1,0:T(1,128)S(1)} all-to-all(f32[8,1,24]{2,1,0:T(1,128)S(1)} %bitcast.97), channel_id=1, replica_groups=mesh['blk'=8,'pix'=4] {'blk'}, dimensions={0} | all-to-all | bytes 1536 | tf_op jit(solution)/shard_map/all_to_all | solution.py:52
  159.9 0.7 reduce.7
  160.7 1.3 gather_fusion.2
  162.4 0.7 fusion.16
  163.1 0.7 fusion.15
  163.8 20.1 %select_select_fusion = f32[192]{0:T(256)S(1)} fusion(pred[192]{0:T(512)(128)(4,1)S(1)} %fusion.11, f32[]{:T(128)} %bitcast.42, f32[]{:T(128)} %bitcast.43, f32[]{:T(128)} %bitcast.44, f32[]{:T(128)} %bitcast.45, f32[]{:T(128)} %bitcast.46, f32[]{:T(128)} %bitcast.47, f32[]{:T(128)} %bitcast.48, f32[]{:T(128)} %bitcast.49, f32[]{:T(128)} %bitcast.50, ...), kind=kLoop, calls=%fused_computation.45 | loop fusion | flops 12096 | bytes 1856 | tf_op jit(solution)/shard_map/jit(_where)/select_n | solution.py:60
  184.0 8.8 %all_to_all.37 = f32[8,1,24]{2,1,0:T(1,128)S(1)} all-to-all(f32[8,1,24]{2,1,0:T(1,128)S(1)} %select_n.91), channel_id=1, replica_groups=mesh['blk'=8,'pix'=4] {'blk'}, dimensions={0} | all-to-all | bytes 1536 | tf_op jit(solution)/shard_map/all_to_all | solution.py:61
  193.2 3.7 %fusion = bf16[288,4096]{1,0:T(8,128)(2,1)} fusion(bf16[8,24,4096]{2,1,0:T(8,128)(2,1)} %all-to-all-done.1, f32[8,24,288]{2,1,0:T(8,128)S(1)} %copy-done.2, f32[288]{0:T(512)S(1)} %fusion.5, f32[288]{0:T(512)S(1)} %fusion.4, f32[8,24]{1,0:T(8,128)S(1)} %bitcast.91, pred[8,24]{1,0:T(8,128)(4,1)S(1)} %compare_bitcast_fusion), kind=kOutput, calls=%fused_computation.4 | convolution fusion | flops 454440960 | bytes 4156608 | tf_op jit(solution)/shard_map/bmt,bmp->tp/dot_general | solution.py:66
  (54 shorter events, 3.2 us)
Async XLA Ops:
  7.2 55.5 %copy-start = (bf16[288,4096]{1,0:T(8,128)(2,1)S(1)}, bf16[288,4096]{1,0:T(8,128)(2,1)}, u32[]{:S(2)}) copy-start(bf16[288,4096]{1,0:T(8,128)(2,1)} %param.6) | copy-start | bytes 7077892
  7.2 1.8 copy-start.1
  14.4 7.5 %copy-start.4 = (s32[32,4]{0,1:T(4,128)S(1)}, s32[32,4]{0,1:T(4,128)}, u32[]{:S(2)}) copy-start(s32[32,4]{0,1:T(4,128)} %param.7) | copy-start | bytes 1540
  14.4 44.5 %all-to-all-start.1 = ((bf16[8,24,4096]{2,1,0:T(8,128)(2,1)}), bf16[8,24,4096]{2,1,0:T(8,128)(2,1)}, u32[]{:S(2)}, u32[]{:S(2)}) async-start(bf16[8,24,4096]{2,1,0:T(8,128)(2,1)} %broadcast_select_fusion), calls=%async_computation.1 | async-start | bytes 3145728 | tf_op jit(solution)/shard_map/all_to_all | solution.py:30
  59.0 10.1 %all-to-all-start = ((bf16[8,1,24]{2,1,0:T(2,128)(2,1)}), bf16[8,1,24]{2,1,0:T(2,128)(2,1)S(1)}, u32[]{:S(2)}, u32[]{:S(2)}) async-start(bf16[8,1,24]{2,1,0:T(2,128)(2,1)} %reshape.347), calls=%async_computation | async-start | bytes 8192 | tf_op jit(solution)/shard_map/all_to_all | solution.py:31
  62.6 39.8 %copy-start.5 = (f32[288]{0:T(512)S(1)}, f32[288]{0:T(512)}, u32[]{:S(2)}) copy-start(f32[288]{0:T(512)} %param.9) | copy-start | bytes 3460
  62.6 37.6 %all-reduce.2.cloned.1.call-start = ((), (), s32[]{:S(2)}) async-start(), calls=%async_computation.6 | async-start | bytes 589824 | tf_op jit(solution)/shard_map/psum | solution.py:35
  66.0 54.2 %copy-start.6 = (f32[32]{0:T(128)S(1)}, f32[32]{0:T(128)}, u32[]{:S(2)}) copy-start(f32[32]{0:T(128)} %param.8) | copy-start | bytes 388
  100.2 50.3 %copy-start.2 = (f32[8,24,288]{2,1,0:T(8,128)S(1)}, f32[8,24,288]{2,1,0:T(8,128)}, u32[]{:S(2)}) copy-start(f32[8,24,288]{2,1,0:T(8,128)} %all-reduce.2.cloned.1.call-done) | copy-start | bytes 663556
  105.3 11.9 %all-to-all-start.2 = ((f32[8,1,24]{2,1,0:T(1,128)}), f32[8,1,24]{2,1,0:T(1,128)S(1)}, u32[]{:S(2)}, u32[]{:S(2)}) async-start(f32[8,1,24]{2,1,0:T(1,128)} %bitcast.5), calls=%async_computation.2 | async-start | bytes 8192 | tf_op jit(solution)/shard_map/all_to_all | solution.py:52
  162.4 34.5 %copy-start.3 = (f32[32]{0:T(128)}, f32[32]{0:T(128)S(1)}, u32[]{:S(2)}) copy-start(f32[32]{0:T(128)S(1)} %log_subtract_fusion.2) | copy-start | bytes 388
Sparse Core Ops, SparseCore 0:
  66.3 33.7 all-reduce.1
where the time goes:
time: 205 us; the launch traced here: 204 us
  waiting for transfers between devices  76.8 us (37%)
  other arithmetic  51.3 us (25%)
  blocking collectives  26.6 us (13%)
  starting transfers between devices  16.6 us (8%)
  between operations  14.3 us (7%)
  local copies, waits for them, and re-layouts  11.1 us (5%)
  matrix products  7.05 us (3%)
    select_n x2, other arithmetic, on_device(): jnp.where(filled, image_duals[owner_image], 0.0).reshape(blocks, capacity)  40 us
    all_to_all x1, waiting for transfers between devices, on_device(): lax.all_to_all(outgoing, 'blk', split_axis=0, concat_axis=0, tiled=True)  36.2 us
    psum x1, waiting for transfers between devices, on_device(): summed = lax.psum(partial_value, 'pix')  31.1 us
    all_to_all x2, blocking collectives, on_device(): lax.all_to_all(duals_send, 'blk', split_axis=0, concat_axis=0, tiled=True)  17.7 us
    all_to_all x1, blocking collectives, on_device(): lax.all_to_all(levels, 'blk', split_axis=0, concat_axis=0, tiled=True)  8.86 us
    all_to_all x1, starting transfers between devices, on_device(): lax.all_to_all(outgoing, 'blk', split_axis=0, concat_axis=0, tiled=True)  7.44 us
    all_to_all x1, waiting for transfers between devices, on_device(): lax.all_to_all(levels, 'blk', split_axis=0, concat_axis=0, tiled=True)  6.41 us
    all_to_all x1, starting transfers between devices, on_device(): lax.all_to_all(levels, 'blk', split_axis=0, concat_axis=0, tiled=True)  5.52 us
  transfers between devices with their start and end apart: 4, of which 4 were waited for; matrix products, arithmetic and copies ran while one was open for 2% of the time, Pallas kernels for 0%

commit v1 on v0

--- a/solution.py
+++ b/solution.py
@@ -4,6 +4,29 @@
 from jax.sharding import PartitionSpec as P
 
 SWEEPS = 2
+
+
+def in_blocks(shard, dim, size):
+    lengths = shard.shape
+    tiles = shard.reshape(*lengths[:dim], size, lengths[dim] // size, *lengths[dim + 1 :])
+    return jnp.moveaxis(tiles, dim, 0)
+
+
+def joined_along(blocks, dim):
+    lengths = list(blocks.shape[1:])
+    lengths[dim] *= blocks.shape[0]
+    return jnp.moveaxis(blocks, 0, dim).reshape(lengths)
+
+
+def sent_to_each(shard, axis, split_dim, concat_dim):
+    peers, index = (lax.axis_size(axis), lax.axis_index(axis))
+    tiles = in_blocks(shard, split_dim, peers)
+    gathered = [tiles[index]]
+    for step in range(1, peers):
+        sent = tiles[(index + step) % peers]
+        gathered.append(lax.ppermute(sent, axis, [(i, (i + step) % peers) for i in range(peers)]))
+    tiles = jnp.stack(gathered)[(index - jnp.arange(peers)) % peers]
+    return joined_along(tiles, concat_dim)
 
 
 def on_device(images, templates, routes, image_weight, template_weight):
@@ -49,7 +72,7 @@
         row_peak = jnp.max(row_terms, axis=2)
         row_total = jnp.sum(jnp.exp(row_terms - row_peak[:, :, None]), axis=2)
         levels = row_peak + jnp.log(row_total)
-        back_levels = lax.all_to_all(levels, "blk", split_axis=0, concat_axis=0, tiled=True)
+        back_levels = sent_to_each(levels, "blk", 0, 0)
         level_routes = back_levels.reshape(-1)[slot_of].reshape(img_dev, admits)
         route_peak = jnp.max(level_routes, axis=1)
         image_duals = (

time: 205 us -> 213 us (1.039)
  starting transfers between devices: 16.6 us -> 30.3 us
  blocking collectives: 26.6 us -> 17.9 us
  waiting for transfers between devices: 76.8 us -> 81.4 us
    ppermute x0 -> x14, starting transfers between devices: none -> 19.2 us  [sent_to_each(): lax.ppermute(sent, axis, [(i, (i + step) % peers) for i in range(peers)])]
    ppermute x0 -> x14, waiting for transfers between devices: none -> 11 us  [sent_to_each(): lax.ppermute(sent, axis, [(i, (i + step) % peers) for i in range(peers)])]
    all_to_all x1 -> x0, blocking collectives: 8.86 us -> none  [on_device(): lax.all_to_all(levels, 'blk', split_axis=0, concat_axis=0, tiled=True)]
    all_to_all x1 -> x0, waiting for transfers between devices: 6.41 us -> none  [on_device(): lax.all_to_all(levels, 'blk', split_axis=0, concat_axis=0, tiled=True)]
    all_to_all x1 -> x0, starting transfers between devices: 5.52 us -> none  [on_device(): lax.all_to_all(levels, 'blk', split_axis=0, concat_axis=0, tiled=True)]
  transfers between devices with their start and end apart: 4 -> 17, of which waited for: 4 -> 9; matrix products, arithmetic and copies ran while one was open for 2% -> 2% of each run, Pallas kernels for 0% -> 0%
where the time goes in v1:
time: 213 us; the launch traced here: 212 us
  waiting for transfers between devices  81.4 us (38%)
  other arithmetic  49.5 us (23%)
  starting transfers between devices  30.3 us (14%)
  blocking collectives  17.9 us (8%)
  between operations  14.4 us (7%)
  local copies, waits for them, and re-layouts  11.8 us (6%)
  matrix products  7.05 us (3%)
    select_n x2, other arithmetic, on_device(): jnp.where(filled, image_duals[owner_image], 0.0).reshape(blocks, capacity)  40.1 us
    all_to_all x1, waiting for transfers between devices, on_device(): lax.all_to_all(outgoing, 'blk', split_axis=0, concat_axis=0, tiled=True)  36.1 us
    psum x1, waiting for transfers between devices, on_device(): summed = lax.psum(partial_value, 'pix')  31.1 us
    ppermute x14, starting transfers between devices, sent_to_each(): lax.ppermute(sent, axis, [(i, (i + step) % peers) for i in range(peers)])  19.2 us
    all_to_all x2, blocking collectives, on_device(): lax.all_to_all(duals_send, 'blk', split_axis=0, concat_axis=0, tiled=True)  17.9 us
    ppermute x14, waiting for transfers between devices, sent_to_each(): lax.ppermute(sent, axis, [(i, (i + step) % peers) for i in range(peers)])  11 us
    all_to_all x1, starting transfers between devices, on_device(): lax.all_to_all(outgoing, 'blk', split_axis=0, concat_axis=0, tiled=True)  7.44 us
  transfers between devices with their start and end apart: 17, of which 9 were waited for; matrix products, arithmetic and copies ran while one was open for 2% of the time, Pallas kernels for 0%

profile of v1, /device:TPU:0, one launch (start us, length us, event | category | flops | bytes accessed | tf_op | source)
XLA Modules:
  0.0 212.3 jit_solution(5009476633730164910)
XLA Ops:
  9.0 2.7 %gather_fusion = bf16[192,4096]{1,0:T(8,128)(2,1)} fusion(bf16[32,4096]{1,0:T(8,128)(2,1)S(1)} %copy-done.1, s32[1024]{0:T(1024)S(1)} %pad_clamp_fusion.2), kind=kCustom, calls=%fused_computation | custom fusion | bytes 3146496 | tf_op jit(solution)/shard_map/gather | solution.py:49
  11.7 2.7 %broadcast_select_fusion = bf16[8,24,4096]{2,1,0:T(8,128)(2,1)} fusion(bf16[8,24,4096]{2,1,0:T(8,128)(2,1)} %bitcast.140, pred[8,24]{1,0:T(8,128)(4,1)S(1)} %broadcast_in_dim.52), kind=kLoop, calls=%fused_computation.9 | loop fusion | flops 786432 | bytes 3145920 | tf_op jit(solution)/shard_map/jit(_where)/select_n | solution.py:49
  14.4 7.4 %all-to-all-start.1 = ((bf16[8,24,4096]{2,1,0:T(8,128)(2,1)}), bf16[8,24,4096]{2,1,0:T(8,128)(2,1)}, u32[]{:S(2)}, u32[]{:S(2)}) async-start(bf16[8,24,4096]{2,1,0:T(8,128)(2,1)} %broadcast_select_fusion), calls=%async_computation.1 | async-start | bytes 3145728 | tf_op jit(solution)/shard_map/all_to_all | solution.py:53
  22.8 36.1 %all-to-all-done.1 = bf16[8,24,4096]{2,1,0:T(8,128)(2,1)} async-done(((bf16[8,24,4096]{2,1,0:T(8,128)(2,1)}), bf16[8,24,4096]{2,1,0:T(8,128)(2,1)}, u32[]{:S(2)}, u32[]{:S(2)}) %all-to-all-start.1) | async-done | bytes 1572896 | tf_op jit(solution)/shard_map/all_to_all | solution.py:53
  59.0 3.6 %all-to-all-start = ((bf16[8,1,24]{2,1,0:T(2,128)(2,1)}), bf16[8,1,24]{2,1,0:T(2,128)(2,1)S(1)}, u32[]{:S(2)}, u32[]{:S(2)}) async-start(bf16[8,1,24]{2,1,0:T(2,128)(2,1)} %reshape.404), calls=%async_computation | async-start | bytes 8192 | tf_op jit(solution)/shard_map/all_to_all | solution.py:54
  62.7 3.3 %fusion.1 = f32[8,24,288]{2,1,0:T(8,128)} fusion(bf16[8,24,4096]{2,1,0:T(8,128)(2,1)} %all-to-all-done.1, bf16[288,4096]{1,0:T(8,128)(2,1)S(1)} %copy-done), kind=kOutput, calls=%fused_computation.7 | convolution fusion | flops 452984832 | bytes 4153344 | tf_op jit(solution)/shard_map/bmp,tp->bmt/dot_general | solution.py:55
  66.0 3.1 %all-to-all-done = bf16[8,1,24]{2,1,0:T(2,128)(2,1)S(1)} async-done(((bf16[8,1,24]{2,1,0:T(2,128)(2,1)}), bf16[8,1,24]{2,1,0:T(2,128)(2,1)S(1)}, u32[]{:S(2)}, u32[]{:S(2)}) %all-to-all-start) | async-done | bytes 416 | tf_op jit(solution)/shard_map/all_to_all | solution.py:54
  69.1 31.1 %all-reduce.2.cloned.1.call-done = f32[8,24,288]{2,1,0:T(8,128)} async-done(((f32[8,24,288]{2,1,0:T(8,128)}), f32[8,24,288]{2,1,0:T(8,128)}) %all-reduce.2.cloned.1.call-update) | async-done | bytes 221200 | tf_op jit(solution)/shard_map/psum | solution.py:58
  100.2 1.1 select_reduce_fusion
  101.3 1.1 exponential_reduce_fusion.3
  102.5 1.1 add_reduce_fusion.1
  103.5 1.2 exponential_reduce_fusion.2
  104.7 4.3 %collective-permute-start.6 = (f32[1,24]{1,0:T(1,128)S(1)}, f32[1,24]{1,0:T(1,128)S(1)}, u32[]{:S(2)}, u32[]{:S(2)}) collective-permute-start(f32[1,24]{1,0:T(1,128)S(1)} %get-tuple-element.10), channel_id=1, source_target_pairs={{0,28},{4,0},{8,4},{12,8},{16,12},{20,16},{24,20},{28,24},{1,29},{... | collective-permute-start | bytes 296 | tf_op jit(solution)/shard_map/ppermute | solution.py:27
  109.6 2.9 %collective-permute-start.3 = (f32[1,24]{1,0:T(1,128)S(1)}, f32[1,24]{1,0:T(1,128)S(1)}, u32[]{:S(2)}, u32[]{:S(2)}) collective-permute-start(f32[1,24]{1,0:T(1,128)S(1)} %get-tuple-element.13), channel_id=1, source_target_pairs={{0,16},{4,20},{8,24},{12,28},{16,0},{20,4},{24,8},{28,12},{1,17},{... | collective-permute-start | bytes 296 | tf_op jit(solution)/shard_map/ppermute | solution.py:27
  112.5 2.0 collective-permute-start.1
  115.5 2.4 %collective-permute-done.2 = f32[1,24]{1,0:T(1,128)S(1)} collective-permute-done((f32[1,24]{1,0:T(1,128)S(1)}, f32[1,24]{1,0:T(1,128)S(1)}, u32[]{:S(2)}, u32[]{:S(2)}) %collective-permute-start.2) | collective-permute-done | bytes 128 | tf_op jit(solution)/shard_map/ppermute | solution.py:27
  118.8 2.0 collective-permute-done
  121.4 1.3 gather_fusion.2
  124.6 20.0 %select_select_fusion.1 = f32[192]{0:T(256)S(1)} fusion(pred[192]{0:T(512)(128)(4,1)S(1)} %fusion.11, f32[]{:T(128)} %bitcast.25, f32[]{:T(128)} %bitcast.26, f32[]{:T(128)} %bitcast.27, f32[]{:T(128)} %bitcast.28, f32[]{:T(128)} %bitcast.29, f32[]{:T(128)} %bitcast.30, f32[]{:T(128)} %bitcast.31, f32[]{:T(128)} %bitcast.32, f32[]{:T(128)} %bitcast.33, ...), kind=kLoop, calls=%fused_computation.69 | loop fusion | flops 12096 | bytes 1856 | tf_op jit(solution)/shard_map/jit(_where)/select_n | solution.py:83
  144.6 9.1 %all_to_all.23 = f32[8,1,24]{2,1,0:T(1,128)S(1)} all-to-all(f32[8,1,24]{2,1,0:T(1,128)S(1)} %select_n.208), channel_id=1, replica_groups=mesh['blk'=8,'pix'=4] {'blk'}, dimensions={0} | all-to-all | bytes 1536 | tf_op jit(solution)/shard_map/all_to_all | solution.py:84
  155.0 1.4 collective-permute-start.12
  156.4 1.5 collective-permute-start.11
  157.9 1.5 collective-permute-start.10
  159.4 1.5 collective-permute-start.9
  160.8 1.5 collective-permute-start.8
  162.9 1.9 collective-permute-done.9
  164.7 1.5 collective-permute-done.8
  166.2 2.4 %collective-permute-done.7 = f32[1,24]{1,0:T(1,128)S(1)} collective-permute-done((f32[1,24]{1,0:T(1,128)S(1)}, f32[1,24]{1,0:T(1,128)S(1)}, u32[]{:S(2)}, u32[]{:S(2)}) %collective-permute-start.7) | collective-permute-done | bytes 128 | tf_op jit(solution)/shard_map/ppermute | solution.py:27
  169.2 1.3 gather_fusion.4
  172.4 20.1 %select_select_fusion = f32[192]{0:T(256)S(1)} fusion(pred[192]{0:T(512)(128)(4,1)S(1)} %fusion.11, f32[]{:T(128)} %bitcast.75, f32[]{:T(128)} %bitcast.76, f32[]{:T(128)} %bitcast.77, f32[]{:T(128)} %bitcast.78, f32[]{:T(128)} %bitcast.79, f32[]{:T(128)} %bitcast.80, f32[]{:T(128)} %bitcast.81, f32[]{:T(128)} %bitcast.82, f32[]{:T(128)} %bitcast.83, ...), kind=kLoop, calls=%fused_computation.68 | loop fusion | flops 12096 | bytes 1856 | tf_op jit(solution)/shard_map/jit(_where)/select_n | solution.py:83
  192.6 8.8 %all_to_all.24 = f32[8,1,24]{2,1,0:T(1,128)S(1)} all-to-all(f32[8,1,24]{2,1,0:T(1,128)S(1)} %select_n.211), channel_id=1, replica_groups=mesh['blk'=8,'pix'=4] {'blk'}, dimensions={0} | all-to-all | bytes 1536 | tf_op jit(solution)/shard_map/all_to_all | solution.py:84
  201.7 3.7 %fusion = bf16[288,4096]{1,0:T(8,128)(2,1)} fusion(bf16[8,24,4096]{2,1,0:T(8,128)(2,1)} %all-to-all-done.1, f32[8,24,288]{2,1,0:T(8,128)S(1)} %copy-done.2, f32[288]{0:T(512)S(1)} %fusion.5, f32[288]{0:T(512)S(1)} %fusion.4, f32[8,24]{1,0:T(8,128)S(1)} %bitcast.145, pred[8,24]{1,0:T(8,128)(4,1)S(1)} %compare_bitcast_fusion), kind=kOutput, calls=%fused_computation.6 | convolution fusion | flops 454440960 | bytes 4156608 | tf_op jit(solution)/shard_map/bmt,bmp->tp/dot_general | solution.py:89
  (84 shorter events, 12.5 us)
Async XLA Ops:
  7.2 55.5 %copy-start = (bf16[288,4096]{1,0:T(8,128)(2,1)S(1)}, bf16[288,4096]{1,0:T(8,128)(2,1)}, u32[]{:S(2)}) copy-start(bf16[288,4096]{1,0:T(8,128)(2,1)} %param.6) | copy-start | bytes 7077892
  7.2 1.8 copy-start.1
  14.4 7.5 %copy-start.4 = (s32[32,4]{0,1:T(4,128)S(1)}, s32[32,4]{0,1:T(4,128)}, u32[]{:S(2)}) copy-start(s32[32,4]{0,1:T(4,128)} %param.7) | copy-start | bytes 1540
  14.4 44.5 %all-to-all-start.1 = ((bf16[8,24,4096]{2,1,0:T(8,128)(2,1)}), bf16[8,24,4096]{2,1,0:T(8,128)(2,1)}, u32[]{:S(2)}, u32[]{:S(2)}) async-start(bf16[8,24,4096]{2,1,0:T(8,128)(2,1)} %broadcast_select_fusion), calls=%async_computation.1 | async-start | bytes 3145728 | tf_op jit(solution)/shard_map/all_to_all | solution.py:53
  59.0 10.1 %all-to-all-start = ((bf16[8,1,24]{2,1,0:T(2,128)(2,1)}), bf16[8,1,24]{2,1,0:T(2,128)(2,1)S(1)}, u32[]{:S(2)}, u32[]{:S(2)}) async-start(bf16[8,1,24]{2,1,0:T(2,128)(2,1)} %reshape.404), calls=%async_computation | async-start | bytes 8192 | tf_op jit(solution)/shard_map/all_to_all | solution.py:54
  62.6 39.8 %copy-start.5 = (f32[288]{0:T(512)S(1)}, f32[288]{0:T(512)}, u32[]{:S(2)}) copy-start(f32[288]{0:T(512)} %param.9) | copy-start | bytes 3460
  62.6 37.6 %all-reduce.2.cloned.1.call-start = ((), (), s32[]{:S(2)}) async-start(), calls=%async_computation.4 | async-start | bytes 589824 | tf_op jit(solution)/shard_map/psum | solution.py:58
  66.0 57.1 %copy-start.6 = (f32[32]{0:T(128)S(1)}, f32[32]{0:T(128)}, u32[]{:S(2)}) copy-start(f32[32]{0:T(128)} %param.8) | copy-start | bytes 388
  100.2 53.5 %copy-start.2 = (f32[8,24,288]{2,1,0:T(8,128)S(1)}, f32[8,24,288]{2,1,0:T(8,128)}, u32[]{:S(2)}) copy-start(f32[8,24,288]{2,1,0:T(8,128)} %all-reduce.2.cloned.1.call-done) | copy-start | bytes 663556
  104.7 7.8 %collective-permute-start.6 = (f32[1,24]{1,0:T(1,128)S(1)}, f32[1,24]{1,0:T(1,128)S(1)}, u32[]{:S(2)}, u32[]{:S(2)}) collective-permute-start(f32[1,24]{1,0:T(1,128)S(1)} %get-tuple-element.10), channel_id=1, source_target_pairs={{0,28},{4,0},{8,4},{12,8},{16,12},{20,16},{24,20},{28,24},{1,29},{... | collective-permute-start | bytes 296 | tf_op jit(solution)/shard_map/ppermute | solution.py:27
  109.0 5.5 %collective-permute-start.5 = (f32[1,24]{1,0:T(1,128)S(1)}, f32[1,24]{1,0:T(1,128)S(1)}, u32[]{:S(2)}, u32[]{:S(2)}) collective-permute-start(f32[1,24]{1,0:T(1,128)S(1)} %get-tuple-element.11), channel_id=1, source_target_pairs={{0,24},{4,28},{8,0},{12,4},{16,8},{20,12},{24,16},{28,20},{1,25},{... | collective-permute-start | bytes 296 | tf_op jit(solution)/shard_map/ppermute | solution.py:27
  109.6 5.9 %collective-permute-start.4 = (f32[1,24]{1,0:T(1,128)S(1)}, f32[1,24]{1,0:T(1,128)S(1)}, u32[]{:S(2)}, u32[]{:S(2)}) collective-permute-start(f32[1,24]{1,0:T(1,128)S(1)} %get-tuple-element.12), channel_id=1, source_target_pairs={{0,20},{4,24},{8,28},{12,0},{16,4},{20,8},{24,12},{28,16},{1,21},{... | collective-permute-start | bytes 296 | tf_op jit(solution)/shard_map/ppermute | solution.py:27
  109.6 5.9 %collective-permute-start.3 = (f32[1,24]{1,0:T(1,128)S(1)}, f32[1,24]{1,0:T(1,128)S(1)}, u32[]{:S(2)}, u32[]{:S(2)}) collective-permute-start(f32[1,24]{1,0:T(1,128)S(1)} %get-tuple-element.13), channel_id=1, source_target_pairs={{0,16},{4,20},{8,24},{12,28},{16,0},{20,4},{24,8},{28,12},{1,17},{... | collective-permute-start | bytes 296 | tf_op jit(solution)/shard_map/ppermute | solution.py:27
  112.5 5.4 %collective-permute-start.2 = (f32[1,24]{1,0:T(1,128)S(1)}, f32[1,24]{1,0:T(1,128)S(1)}, u32[]{:S(2)}, u32[]{:S(2)}) collective-permute-start(f32[1,24]{1,0:T(1,128)S(1)} %get-tuple-element.14), channel_id=1, source_target_pairs={{0,12},{4,16},{8,20},{12,24},{16,28},{20,0},{24,4},{28,8},{1,13},{... | collective-permute-start | bytes 296 | tf_op jit(solution)/shard_map/ppermute | solution.py:27
  112.5 6.3 %collective-permute-start.1 = (f32[1,24]{1,0:T(1,128)S(1)}, f32[1,24]{1,0:T(1,128)S(1)}, u32[]{:S(2)}, u32[]{:S(2)}) collective-permute-start(f32[1,24]{1,0:T(1,128)S(1)} %get-tuple-element.15), channel_id=1, source_target_pairs={{0,8},{4,12},{8,16},{12,20},{16,24},{20,28},{24,0},{28,4},{1,9},{5... | collective-permute-start | bytes 296 | tf_op jit(solution)/shard_map/ppermute | solution.py:27
  114.5 6.3 %collective-permute-start = (f32[1,24]{1,0:T(1,128)S(1)}, f32[1,24]{1,0:T(1,128)S(1)}, u32[]{:S(2)}, u32[]{:S(2)}) collective-permute-start(f32[1,24]{1,0:T(1,128)S(1)} %get-tuple-element.16), channel_id=1, source_target_pairs={{0,4},{4,8},{8,12},{12,16},{16,20},{20,24},{24,28},{28,0},{1,5},{5... | collective-permute-start | bytes 296 | tf_op jit(solution)/shard_map/ppermute | solution.py:27
  154.4 6.5 %collective-permute-start.13 = (f32[1,24]{1,0:T(1,128)S(1)}, f32[1,24]{1,0:T(1,128)S(1)}, u32[]{:S(2)}, u32[]{:S(2)}) collective-permute-start(f32[1,24]{1,0:T(1,128)S(1)} %get-tuple-element.2), channel_id=1, source_target_pairs={{0,28},{4,0},{8,4},{12,8},{16,12},{20,16},{24,20},{28,24},{1,29},{... | collective-permute-start | bytes 296 | tf_op jit(solution)/shard_map/ppermute | solution.py:27
  155.0 7.3 %collective-permute-start.12 = (f32[1,24]{1,0:T(1,128)S(1)}, f32[1,24]{1,0:T(1,128)S(1)}, u32[]{:S(2)}, u32[]{:S(2)}) collective-permute-start(f32[1,24]{1,0:T(1,128)S(1)} %get-tuple-element.3), channel_id=1, source_target_pairs={{0,24},{4,28},{8,0},{12,4},{16,8},{20,12},{24,16},{28,20},{1,25},{... | collective-permute-start | bytes 296 | tf_op jit(solution)/shard_map/ppermute | solution.py:27
  156.4 6.4 %collective-permute-start.11 = (f32[1,24]{1,0:T(1,128)S(1)}, f32[1,24]{1,0:T(1,128)S(1)}, u32[]{:S(2)}, u32[]{:S(2)}) collective-permute-start(f32[1,24]{1,0:T(1,128)S(1)} %get-tuple-element.4), channel_id=1, source_target_pairs={{0,20},{4,24},{8,28},{12,0},{16,4},{20,8},{24,12},{28,16},{1,21},{... | collective-permute-start | bytes 296 | tf_op jit(solution)/shard_map/ppermute | solution.py:27
  157.9 5.0 %collective-permute-start.10 = (f32[1,24]{1,0:T(1,128)S(1)}, f32[1,24]{1,0:T(1,128)S(1)}, u32[]{:S(2)}, u32[]{:S(2)}) collective-permute-start(f32[1,24]{1,0:T(1,128)S(1)} %get-tuple-element.5), channel_id=1, source_target_pairs={{0,16},{4,20},{8,24},{12,28},{16,0},{20,4},{24,8},{28,12},{1,17},{... | collective-permute-start | bytes 296 | tf_op jit(solution)/shard_map/ppermute | solution.py:27
  159.4 5.4 %collective-permute-start.9 = (f32[1,24]{1,0:T(1,128)S(1)}, f32[1,24]{1,0:T(1,128)S(1)}, u32[]{:S(2)}, u32[]{:S(2)}) collective-permute-start(f32[1,24]{1,0:T(1,128)S(1)} %get-tuple-element.6), channel_id=1, source_target_pairs={{0,12},{4,16},{8,20},{12,24},{16,28},{20,0},{24,4},{28,8},{1,13},{... | collective-permute-start | bytes 296 | tf_op jit(solution)/shard_map/ppermute | solution.py:27
  160.8 5.4 %collective-permute-start.8 = (f32[1,24]{1,0:T(1,128)S(1)}, f32[1,24]{1,0:T(1,128)S(1)}, u32[]{:S(2)}, u32[]{:S(2)}) collective-permute-start(f32[1,24]{1,0:T(1,128)S(1)} %get-tuple-element.7), channel_id=1, source_target_pairs={{0,8},{4,12},{8,16},{12,20},{16,24},{20,28},{24,0},{28,4},{1,9},{5... | collective-permute-start | bytes 296 | tf_op jit(solution)/shard_map/ppermute | solution.py:27
  162.3 6.3 %collective-permute-start.7 = (f32[1,24]{1,0:T(1,128)S(1)}, f32[1,24]{1,0:T(1,128)S(1)}, u32[]{:S(2)}, u32[]{:S(2)}) collective-permute-start(f32[1,24]{1,0:T(1,128)S(1)} %get-tuple-element.8), channel_id=1, source_target_pairs={{0,4},{4,8},{8,12},{12,16},{16,20},{20,24},{24,28},{28,0},{1,5},{5... | collective-permute-start | bytes 296 | tf_op jit(solution)/shard_map/ppermute | solution.py:27
  170.9 34.5 %copy-start.3 = (f32[32]{0:T(128)}, f32[32]{0:T(128)S(1)}, u32[]{:S(2)}) copy-start(f32[32]{0:T(128)S(1)} %log_subtract_fusion.2) | copy-start | bytes 388
Sparse Core Ops, SparseCore 0:
  66.3 33.7 all-reduce.1
